TPU v7x, 512 devices: a whole 4x4x16 slice. The times are simulated.
512 devices in a mesh: lat: 4 (over x_hi, core), lon: 32 (over z, x_lo), tensor: 4 (over y).
Axes of the slice: x: 4 (x_hi: 2, x_lo: 2; x = x_hi * 2 + x_lo), y: 4, z: 16, core: 2. Of those that a mesh axis runs over, the one named last changes fastest.
Arguments:
- fields: bfloat16 [64, 768, 256], P('lat', 'lon'), may hold values from -8 to 8
- norm_gain1: float32 [256], replicated, may hold values from 0.5 to 1.5
- w_qkv: bfloat16 [256, 3, 8, 32], P(None, None, 'tensor'), may hold values from -0.1875 to 0.1875
- logit_scale: float32 [8], P('tensor'), may hold values from 1 to 64
- w_out: bfloat16 [8, 32, 256], P('tensor'), may hold values from -0.375 to 0.375
- attn_keep: int32 [64, 256], P('lat'), may hold values 0 or 1
- dw_kernel: bfloat16 [7, 7, 256], replicated, may hold values from -0.875 to 0.875
- norm_gain2: float32 [256], replicated, may hold values from 0.5 to 1.5
- w_up: bfloat16 [256, 1024], P(None, 'tensor'), may hold values from -0.375 to 0.375
- w_down: bfloat16 [1024, 256], P('tensor'), may hold values from -0.1875 to 0.1875
- mlp_keep: int32 [64, 256], P('lat'), may hold values 0 or 1
Outputs:
- result: bfloat16 [64, 768, 256], P('lat', 'lon')
All inputs are finite; a program needn't handle non-finite values. No bound on the sum of `attn_keep` or of `mlp_keep` on one device may be relied on, other than what follows from the above.
Results may differ from a plain program's by a relative error of at most 0.014.
Values may be sent and summed in bfloat16 or wider, within the bound.
A program may use at most 64 MiB of HBM per device.

v0:
```python
import math
import jax
import jax.numpy as jnp
from jax import lax
from jax.sharding import PartitionSpec as P

ln_eps = 1e-05
keep_prob = 0.9


def padded(shard, sides, width, wrap):
    for axis, dim in sides:
        size, length = (lax.axis_size(axis), shard.shape[dim])
        up = [(i, (i + 1) % size) for i in range(size if wrap else size - 1)]
        down = [(j, i) for i, j in up]
        last = lax.slice_in_dim(shard, length - width, length, axis=dim)
        first = lax.slice_in_dim(shard, 0, width, axis=dim)
        before = lax.ppermute(last, axis, up)
        after = lax.ppermute(first, axis, down)
        shard = jnp.concatenate([before, shard, after], axis=dim)
    return shard


def layer_norm(values, gain):
    widened = values.astype(jnp.float32)
    center = jnp.mean(widened, axis=-1, keepdims=True)
    spread = jnp.mean(jnp.square(widened - center), axis=-1, keepdims=True)
    return (widened - center) * lax.rsqrt(spread + ln_eps) * gain


def depthwise(wide, kernel, rows, cols):
    kernel_f = kernel.astype(jnp.float32)
    wide_f = wide.astype(jnp.float32)
    width = kernel.shape[0]
    total = jnp.zeros((rows, cols, wide.shape[2]), jnp.float32)
    for row_off in range(width):
        for col_off in range(width):
            total = (
                total
                + kernel_f[row_off, col_off]
                * wide_f[row_off : row_off + rows, col_off : col_off + cols]
            )
    return total


def widen(stream, margin):
    rows_wide = padded(stream, (("lat", 0),), margin, False)
    return padded(rows_wide, (("lon", 1),), margin, True)


def feed_forward(spatial, norm_gain2, w_up, w_down):
    normed2 = layer_norm(spatial, norm_gain2).astype(jnp.bfloat16)
    hidden = jax.nn.gelu(
        jnp.einsum("rlc,cf->rlf", normed2, w_up, preferred_element_type=jnp.float32),
        approximate=False,
    ).astype(jnp.bfloat16)
    return jnp.einsum("rlf,fc->rlc", hidden, w_down, preferred_element_type=jnp.float32)


def shards(
    fields,
    norm_gain1,
    w_qkv,
    logit_scale,
    w_out,
    attn_keep,
    dw_kernel,
    norm_gain2,
    w_up,
    w_down,
    mlp_keep,
):
    lat_rows, lon_cols, channels = fields.shape
    local_heads = w_qkv.shape[2]
    head_size = w_qkv.shape[3]
    logit_coef = logit_scale * (1.0 / math.sqrt(head_size))
    normed = layer_norm(fields, norm_gain1).astype(jnp.bfloat16)
    projected = jnp.einsum(
        "rlc,cjhd->rljhd", normed, w_qkv, preferred_element_type=jnp.float32
    ).astype(jnp.bfloat16)
    queries = projected[:, :, 0]
    keys_values = projected[:, :, 1:].reshape(lat_rows, lon_cols, 2 * local_heads * head_size)
    piece = lax.all_gather(keys_values, "lon", axis=1, tiled=True)
    running_max = jnp.full((lat_rows, local_heads, lon_cols), -1e30, jnp.float32)
    count = piece.shape[1]
    split_piece = piece.reshape(lat_rows, count, 2, local_heads, head_size)
    scores = jnp.einsum(
        "rqhd,rkhd->rhqk", queries, split_piece[:, :, 0], preferred_element_type=jnp.float32
    )
    scores = scores * logit_coef[None, :, None, None]
    new_max = jnp.maximum(running_max, jnp.max(scores, axis=-1))
    weights = jnp.exp(scores - new_max[..., None])
    new_sum = jnp.sum(weights, axis=-1)
    gathered = jnp.einsum(
        "rhqk,rkhd->rhqd",
        weights.astype(jnp.bfloat16),
        split_piece[:, :, 1],
        preferred_element_type=jnp.float32,
    )
    mixed = (gathered / new_sum[..., None]).astype(jnp.bfloat16)
    partial_value = jnp.einsum("rhqd,hdc->rqc", mixed, w_out, preferred_element_type=jnp.float32)
    attended = lax.psum(partial_value.astype(jnp.bfloat16), "tensor").astype(jnp.float32)
    attn_factor = (attn_keep.astype(jnp.float32) / keep_prob)[:, None, :]
    mlp_factor = (mlp_keep.astype(jnp.float32) / keep_prob)[:, None, :]
    margin = dw_kernel.shape[0] // 2
    stream = (fields.astype(jnp.float32) + attended * attn_factor).astype(jnp.bfloat16)
    spatial = depthwise(widen(stream, margin), dw_kernel, lat_rows, lon_cols).astype(jnp.bfloat16)
    ffn_sum = lax.psum(
        feed_forward(spatial, norm_gain2, w_up, w_down).astype(jnp.bfloat16), "tensor"
    ).astype(jnp.float32)
    result = (stream.astype(jnp.float32) + ffn_sum * mlp_factor).astype(jnp.bfloat16)
    return result


def solution(mesh):
    placed = (
        P("lat", "lon", None),
        P(),
        P(None, None, "tensor", None),
        P("tensor"),
        P("tensor", None, None),
        P("lat", None),
        P(),
        P(),
        P(None, "tensor"),
        P("tensor", None),
        P("lat", None),
    )
    return jax.shard_map(
        shards, mesh=mesh, in_specs=placed, out_specs=P("lat", "lon", None), check_vma=False
    )
```

profile of v0, /device:TPU:2, one launch (start us, length us, event | category | flops | bytes accessed | tf_op | source)
XLA Modules:
  0.0 309.6 jit_solution(4489916328786344057)
XLA Ops:
  6.5 1.1 convert_reduce_fusion
  7.7 1.2 fusion.18
  8.8 1.4 convolution_convert_fusion
  10.3 0.3 copy.12
  10.6 0.9 reshape.39
  11.5 0.0 all-gather.2.cloned.1.call-update
  11.5 0.0 all-reduce.3.cloned.1.call-start
  11.6 140.8 %all-gather.2.cloned.1.call-done = bf16[16,768,128]{2,1,0:T(8,128)(2,1)} async-done(((bf16[16,24,128]{2,1,0:T(8,128)(2,1)}), bf16[16,768,128]{2,1,0:T(8,128)(2,1)}) %all-gather.2.cloned.1.call-update) | async-done | bytes 3145744 | tf_op jit(solution)/shard_map/all_gather | solution.py:83
  152.4 4.7 %copy.13 = bf16[16,768,128]{1,2,0:T(8,128)(2,1)} copy(bf16[16,768,128]{2,1,0:T(8,128)(2,1)} %all-gather.2.cloned.1.call-done) | data formatting | bytes 6291456 | tf_op jit(solution)/shard_map/all_gather | solution.py:83
  157.1 2.0 multiply_reduce_fusion
  159.0 0.6 fusion
  159.7 0.0 copy-start.2
  159.7 0.0 copy-start.1
  159.7 3.2 %fusion.11 = bf16[16,24,256]{2,1,0:T(8,128)(2,1)} fusion(bf16[16,768,2,2,32]{1,4,3,2,0:T(8,128)(2,1)} %bitcast.96, f32[16,2,24,768]{3,2,1,0:T(8,128)S(1)} %get-tuple-element.63, f32[16,2,24]{2,1,0:T(2,128)S(1)} %broadcast_maximum_fusion, f32[2]{0:T(128)S(1)} %broadcast_multiply_fusion.2, f32[16,2,24]{2,1,0:T(2,128)S(1)} %fusion, ...), kind=kOutput, calls=%fused_computation.14 | convolution fusion | flops 52248576 | bytes 4167688 | tf_op jit(solution)/shard_map/rhqd,hdc->rqc/dot_general | solution.py:101
  162.9 0.0 all-reduce.3.cloned.1.call-update
  162.9 0.0 all-reduce.5.cloned.1.call-start
  163.0 54.8 %all-reduce.3.cloned.1.call-done = bf16[16,24,256]{2,1,0:T(8,128)(2,1)} async-done(((bf16[16,24,256]{2,1,0:T(8,128)(2,1)}), bf16[16,24,256]{2,1,0:T(8,128)(2,1)}) %all-reduce.3.cloned.1.call-update) | async-done | bytes 196624 | tf_op jit(solution)/shard_map/psum | solution.py:102
  217.8 1.0 fusion.24
  218.8 1.3 collective-permute-start
  220.1 1.3 collective-permute-start.1
  221.5 4.1 %collective-permute-done.1 = bf16[3,24,256]{2,1,0:T(8,128)(2,1)S(1)} collective-permute-done((bf16[3,24,256]{2,1,0:T(8,128)(2,1)S(1)}, bf16[3,24,256]{2,1,0:T(8,128)(2,1)S(1)}, u32[]{:S(2)}, u32[]{:S(2)}) %collective-permute-start.1) | collective-permute-done | bytes 36896 | tf_op jit(solution)/shard_map/ppermute | solution.py:19
  225.6 4.4 %collective-permute-start.2 = (bf16[22,3,256]{2,1,0:T(4,128)(2,1)S(1)}, bf16[22,3,256]{2,1,0:T(4,128)(2,1)S(1)}, u32[]{:S(2)}, u32[]{:S(2)}) collective-permute-start(bf16[22,3,256]{2,1,0:T(4,128)(2,1)S(1)} %get-tuple-element.9), channel_id=1, source_target_pairs={{0,4},{4,8},{8,12},{12,16},{16,20},{20,24},{24,28},{28,32},{32,36}... | collective-permute-start | bytes 101384 | tf_op jit(solution)/shard_map/ppermute | solution.py:18
  230.0 1.9 collective-permute-start.3
  231.9 4.9 %collective-permute-done.3 = bf16[22,3,256]{2,1,0:T(4,128)(2,1)S(1)} collective-permute-done((bf16[22,3,256]{2,1,0:T(4,128)(2,1)S(1)}, bf16[22,3,256]{2,1,0:T(4,128)(2,1)S(1)}, u32[]{:S(2)}, u32[]{:S(2)}) %collective-permute-start.3) | collective-permute-done | bytes 33824 | tf_op jit(solution)/shard_map/ppermute | solution.py:19
  236.8 0.1 maximum_convert_fusion
  237.0 2.9 convert_reduce_fusion.1
  239.9 0.2 fusion.21
  240.2 0.3 fusion.95
  240.5 1.8 convolution_convert_fusion.1
  242.3 0.0 all-reduce.5.cloned.1.call-update
  242.3 59.0 %all-reduce.5.cloned.1.call-done = bf16[16,24,256]{2,1,0:T(8,128)(2,1)} async-done(((bf16[16,24,256]{2,1,0:T(8,128)(2,1)}), bf16[16,24,256]{2,1,0:T(8,128)(2,1)}) %all-reduce.5.cloned.1.call-update) | async-done | bytes 196624 | tf_op jit(solution)/shard_map/psum | solution.py:108
  301.4 1.7 add_convert_fusion
  (33 shorter events, 0.2 us)
Async XLA Ops:
  6.5 233.6 %copy-start = (bf16[256,256]{1,0:T(8,128)(2,1)S(1)}, bf16[256,256]{1,0:T(8,128)(2,1)}, u32[]{:S(2)}) copy-start(bf16[256,256]{1,0:T(8,128)(2,1)} %param.19) | copy-start | bytes 393220
  6.5 5.0 %copy-start.8 = (f32[2]{0:T(128)S(1)}, f32[2]{0:T(128)}, u32[]{:S(2)}) copy-start(f32[2]{0:T(128)} %param.14) | copy-start | bytes 28
  6.5 5.0 %copy-start.3 = (s32[16,256]{1,0:T(8,128)S(1)}, s32[16,256]{1,0:T(8,128)}, u32[]{:S(2)}) copy-start(s32[16,256]{1,0:T(8,128)} %param.16) | copy-start | bytes 49156
  6.5 145.8 %all-gather.2.cloned.1.call-start = ((), (), s32[]{:S(2)}) async-start(), calls=%async_computation | async-start | bytes 3244032 | tf_op jit(solution)/shard_map/all_gather | solution.py:83
  11.5 206.3 %all-reduce.3.cloned.1.call-start = ((), (), s32[]{:S(2)}) async-start(), calls=%async_computation.1 | async-start | bytes 393216 | tf_op jit(solution)/shard_map/psum | solution.py:102
  157.0 2.6 copy-start.6
  159.7 3.3 %copy-start.2 = (bf16[7,7,256]{2,1,0:T(8,128)(2,1)S(1)}, bf16[7,7,256]{2,1,0:T(8,128)(2,1)}, u32[]{:S(2)}) copy-start(bf16[7,7,256]{2,1,0:T(8,128)(2,1)} %param.17) | copy-start | bytes 75268
  159.7 58.2 %copy-start.1 = (bf16[16,24,256]{2,1,0:T(8,128)(2,1)S(1)}, bf16[16,24,256]{2,1,0:T(8,128)(2,1)}, u32[]{:S(2)}) copy-start(bf16[16,24,256]{2,1,0:T(8,128)(2,1)} %param.11) | copy-start | bytes 589828
  162.9 138.5 %all-reduce.5.cloned.1.call-start = ((), (), s32[]{:S(2)}) async-start(), calls=%async_computation.2 | async-start | bytes 393216 | tf_op jit(solution)/shard_map/psum | solution.py:108
  218.8 2.6 collective-permute-start
  220.1 5.4 %collective-permute-start.1 = (bf16[3,24,256]{2,1,0:T(8,128)(2,1)S(1)}, bf16[3,24,256]{2,1,0:T(8,128)(2,1)S(1)}, u32[]{:S(2)}, u32[]{:S(2)}) collective-permute-start(bf16[3,24,256]{2,1,0:T(8,128)(2,1)S(1)} %get-tuple-element.12), channel_id=1, source_target_pairs={{128,0},{256,128},{384,256},{129,1},{257,129},{385,257},{130,2},{2... | collective-permute-start | bytes 110600 | tf_op jit(solution)/shard_map/ppermute | solution.py:19
  225.6 6.3 %collective-permute-start.2 = (bf16[22,3,256]{2,1,0:T(4,128)(2,1)S(1)}, bf16[22,3,256]{2,1,0:T(4,128)(2,1)S(1)}, u32[]{:S(2)}, u32[]{:S(2)}) collective-permute-start(bf16[22,3,256]{2,1,0:T(4,128)(2,1)S(1)} %get-tuple-element.9), channel_id=1, source_target_pairs={{0,4},{4,8},{8,12},{12,16},{16,20},{20,24},{24,28},{28,32},{32,36}... | collective-permute-start | bytes 101384 | tf_op jit(solution)/shard_map/ppermute | solution.py:18
  230.0 6.8 %collective-permute-start.3 = (bf16[22,3,256]{2,1,0:T(4,128)(2,1)S(1)}, bf16[22,3,256]{2,1,0:T(4,128)(2,1)S(1)}, u32[]{:S(2)}, u32[]{:S(2)}) collective-permute-start(bf16[22,3,256]{2,1,0:T(4,128)(2,1)S(1)} %get-tuple-element.10), channel_id=1, source_target_pairs={{4,0},{8,4},{12,8},{16,12},{20,16},{24,20},{28,24},{32,28},{36,32}... | collective-permute-start | bytes 101384 | tf_op jit(solution)/shard_map/ppermute | solution.py:19
  236.9 3.2 %copy-start.7 = (f32[256]{0:T(256)S(1)}, f32[256]{0:T(256)}, u32[]{:S(2)}) copy-start(f32[256]{0:T(256)} %param.18) | copy-start | bytes 3076
  237.0 3.6 %copy-start.5 = (bf16[256,256]{1,0:T(8,128)(2,1)S(1)}, bf16[256,256]{1,0:T(8,128)(2,1)}, u32[]{:S(2)}) copy-start(bf16[256,256]{1,0:T(8,128)(2,1)} %param.20) | copy-start | bytes 393220
  240.5 1.8 copy-start.4
Sparse Core Ops, SparseCore 0:
  11.6 140.6 all-gather.1
  163.0 54.7 all-reduce.2
  242.4 58.8 all-reduce.4
where the time goes:
time: 310 us
  waiting for transfers between devices  264 us (85%)
  between operations  13.4 us (4%)
  starting transfers between devices  8.95 us (3%)
  other arithmetic  8.84 us (3%)
  matrix products  8.69 us (3%)
  local copies, waits for them, and re-layouts  6.01 us (2%)
    all_gather x1, waiting for transfers between devices, shards(): piece = lax.all_gather(keys_values, 'lon', axis=1, tiled=True)  141 us
    psum x1, waiting for transfers between devices, shards(): lax.psum(feed_forward(spatial, norm_gain2, w_up, w_down).astype(jnp.bfloa...  59 us
    psum x1, waiting for transfers between devices, shards(): lax.psum(partial_value.astype(jnp.bfloat16), 'tensor').astype(jnp.float32)  54.8 us
    ppermute x2, waiting for transfers between devices, padded(): after = lax.ppermute(first, axis, down)  8.96 us
  transfers between devices with their start and end apart: 7, of which 5 were waited for; matrix products, arithmetic and copies ran while one was open for 0% of the time, Pallas kernels for 0%

commit v1 on v0

--- a/solution.py
+++ b/solution.py
@@ -6,6 +6,10 @@
 
 ln_eps = 1e-05
 keep_prob = 0.9
+
+
+def answer_side(arr_in, chip_axis):
+    return lax.all_gather(arr_in, chip_axis).sum(axis=0)
 
 
 def padded(shard, sides, width, wrap):
@@ -99,7 +103,7 @@
     )
     mixed = (gathered / new_sum[..., None]).astype(jnp.bfloat16)
     partial_value = jnp.einsum("rhqd,hdc->rqc", mixed, w_out, preferred_element_type=jnp.float32)
-    attended = lax.psum(partial_value.astype(jnp.bfloat16), "tensor").astype(jnp.float32)
+    attended = answer_side(partial_value.astype(jnp.bfloat16), "tensor").astype(jnp.float32)
     attn_factor = (attn_keep.astype(jnp.float32) / keep_prob)[:, None, :]
     mlp_factor = (mlp_keep.astype(jnp.float32) / keep_prob)[:, None, :]
     margin = dw_kernel.shape[0] // 2

time: 310 us -> 264 us (0.85)
  waiting for transfers between devices: 264 us -> 206 us
  blocking collectives: 0 us -> 13.4 us
    psum x1 -> x0, waiting for transfers between devices: 54.8 us -> none  [shards(): lax.psum(partial_value.astype(jnp.bfloat16), 'tensor').astype(jnp.float32)]
    all_gather x0 -> x1, blocking collectives: none -> 13.4 us  [answer_side(): return lax.all_gather(arr_in, chip_axis).sum(axis=0)]
    psum x1, waiting for transfers between devices: 59 us -> 55.8 us  [shards(): lax.psum(feed_forward(spatial, norm_gain2, w_up, w_down).astype(jnp.bfloa...]
  transfers between devices with their start and end apart: 7 -> 6, of which waited for: 5 -> 4; matrix products, arithmetic and copies ran while one was open for 0% -> 0% of each run, Pallas kernels for 0% -> 0%
where the time goes in v1:
time: 264 us
  waiting for transfers between devices  206 us (78%)
  between operations  13.7 us (5%)
  blocking collectives  13.4 us (5%)
  starting transfers between devices  9.03 us (3%)
  other arithmetic  8.05 us (3%)
  matrix products  7.99 us (3%)
  local copies, waits for them, and re-layouts  6.01 us (2%)
    all_gather x1, waiting for transfers between devices, shards(): piece = lax.all_gather(keys_values, 'lon', axis=1, tiled=True)  141 us
    psum x1, waiting for transfers between devices, shards(): lax.psum(feed_forward(spatial, norm_gain2, w_up, w_down).astype(jnp.bfloa...  55.8 us
    all_gather x1, blocking collectives, answer_side(): return lax.all_gather(arr_in, chip_axis).sum(axis=0)  13.4 us
    ppermute x2, waiting for transfers between devices, padded(): after = lax.ppermute(first, axis, down)  9.23 us
    ppermute x2, starting transfers between devices, padded(): before = lax.ppermute(last, axis, up)  5.74 us
  transfers between devices with their start and end apart: 6, of which 4 were waited for; matrix products, arithmetic and copies ran while one was open for 0% of the time, Pallas kernels for 0%

profile of v1, /device:TPU:2, one launch (start us, length us, event | category | flops | bytes accessed | tf_op | source)
XLA Modules:
  0.0 264.0 jit_solution(16548858310695219353)
XLA Ops:
  6.5 0.0 all-gather.3.cloned.1.call-start
  6.6 1.1 convert_reduce_fusion
  7.7 1.2 fusion.18
  8.9 1.4 convolution_convert_fusion
  10.3 0.3 copy.15
  10.6 0.9 reshape.39
  11.5 0.0 all-gather.3.cloned.1.call-update
  11.5 0.0 all-reduce.2.cloned.1.call-start
  11.7 140.7 %all-gather.3.cloned.1.call-done = bf16[16,768,128]{2,1,0:T(8,128)(2,1)} async-done(((bf16[16,24,128]{2,1,0:T(8,128)(2,1)}), bf16[16,768,128]{2,1,0:T(8,128)(2,1)}) %all-gather.3.cloned.1.call-update) | async-done | bytes 3145744 | tf_op jit(solution)/shard_map/all_gather | solution.py:87
  152.4 4.7 %copy.16 = bf16[16,768,128]{1,2,0:T(8,128)(2,1)} copy(bf16[16,768,128]{2,1,0:T(8,128)(2,1)} %all-gather.3.cloned.1.call-done) | data formatting | bytes 6291456 | tf_op jit(solution)/shard_map/all_gather | solution.py:87
  157.1 2.0 multiply_reduce_fusion
  159.1 0.6 fusion
  159.7 2.5 fusion.11
  162.2 13.4 %all-gather = bf16[64,24,256]{2,1,0:T(8,128)(2,1)S(1)} all-gather(bf16[16,24,256]{2,1,0:T(8,128)(2,1)S(1)} %fusion.11), channel_id=2, replica_groups=mesh['lat'=4,'lon'=32,'tensor'=4] {'tensor'}, dimensions={0}, use_global_device_ids=true | all-gather | bytes 983040 | tf_op jit(solution)/shard_map/all_gather | solution.py:12
  175.6 0.1 reduce_sum.60
  175.7 0.1 fusion.24
  175.8 1.3 collective-permute-start
  177.1 1.3 collective-permute-start.1
  178.5 4.4 %collective-permute-done.1 = bf16[3,24,256]{2,1,0:T(8,128)(2,1)S(1)} collective-permute-done((bf16[3,24,256]{2,1,0:T(8,128)(2,1)S(1)}, bf16[3,24,256]{2,1,0:T(8,128)(2,1)S(1)}, u32[]{:S(2)}, u32[]{:S(2)}) %collective-permute-start.1) | collective-permute-done | bytes 36896 | tf_op jit(solution)/shard_map/ppermute | solution.py:23
  182.9 4.4 %collective-permute-start.2 = (bf16[22,3,256]{2,1,0:T(4,128)(2,1)S(1)}, bf16[22,3,256]{2,1,0:T(4,128)(2,1)S(1)}, u32[]{:S(2)}, u32[]{:S(2)}) collective-permute-start(bf16[22,3,256]{2,1,0:T(4,128)(2,1)S(1)} %get-tuple-element.9), channel_id=1, source_target_pairs={{0,4},{4,8},{8,12},{12,16},{16,20},{20,24},{24,28},{28,32},{32,36}... | collective-permute-start | bytes 101384 | tf_op jit(solution)/shard_map/ppermute | solution.py:22
  187.3 1.9 collective-permute-start.3
  189.3 4.9 %collective-permute-done.3 = bf16[22,3,256]{2,1,0:T(4,128)(2,1)S(1)} collective-permute-done((bf16[22,3,256]{2,1,0:T(4,128)(2,1)S(1)}, bf16[22,3,256]{2,1,0:T(4,128)(2,1)S(1)}, u32[]{:S(2)}, u32[]{:S(2)}) %collective-permute-start.3) | collective-permute-done | bytes 33824 | tf_op jit(solution)/shard_map/ppermute | solution.py:23
  194.2 0.1 maximum_convert_fusion
  194.3 0.0 copy-start.7
  194.3 0.0 copy-start.5
  194.3 2.9 %convert_reduce_fusion.1 = (f32[16,24]{1,0:T(8,128)S(1)}, bf16[16,24,256]{2,1,0:T(8,128)(2,1)S(1)}) fusion(f32[22,30,256]{2,1,0:T(8,128)S(1)} %maximum_convert_fusion, f32[256]{0:T(256)S(1)} %bitcast.149, f32[256]{0:T(256)S(1)} %bitcast.148, f32[256]{0:T(256)S(1)} %bitcast.147, f32[256]{0:T(256)S(1)} %bitcast.146, f32[256]{0:T(256)S(1)} %bitcast.145, ...), kind=kLoop, calls=%fused_computation.21 | loop fusion | flops 9830016 | bytes 19515904 | tf_op jit(solution)/shard_map/reduce_sum | solution.py:30
  197.2 0.2 fusion.21
  197.5 0.3 fusion.95
  197.9 1.8 convolution_convert_fusion.1
  199.7 0.0 all-reduce.2.cloned.1.call-update
  199.7 55.8 %all-reduce.2.cloned.1.call-done = bf16[16,24,256]{2,1,0:T(8,128)(2,1)} async-done(((bf16[16,24,256]{2,1,0:T(8,128)(2,1)}), bf16[16,24,256]{2,1,0:T(8,128)(2,1)}) %all-reduce.2.cloned.1.call-update) | async-done | bytes 196624 | tf_op jit(solution)/shard_map/psum | solution.py:112
  255.5 1.7 add_convert_fusion
  (32 shorter events, 0.2 us)
Async XLA Ops:
  6.5 191.0 %copy-start = (bf16[256,256]{1,0:T(8,128)(2,1)S(1)}, bf16[256,256]{1,0:T(8,128)(2,1)}, u32[]{:S(2)}) copy-start(bf16[256,256]{1,0:T(8,128)(2,1)} %param.19) | copy-start | bytes 393220
  6.5 5.0 %copy-start.8 = (f32[2]{0:T(128)S(1)}, f32[2]{0:T(128)}, u32[]{:S(2)}) copy-start(f32[2]{0:T(128)} %param.14) | copy-start | bytes 28
  6.5 5.1 %copy-start.2 = (bf16[7,7,256]{2,1,0:T(8,128)(2,1)S(1)}, bf16[7,7,256]{2,1,0:T(8,128)(2,1)}, u32[]{:S(2)}) copy-start(bf16[7,7,256]{2,1,0:T(8,128)(2,1)} %param.17) | copy-start | bytes 75268
  6.5 5.1 %copy-start.3 = (s32[16,256]{1,0:T(8,128)S(1)}, s32[16,256]{1,0:T(8,128)}, u32[]{:S(2)}) copy-start(s32[16,256]{1,0:T(8,128)} %param.16) | copy-start | bytes 49156
  6.5 145.8 %all-gather.3.cloned.1.call-start = ((), (), s32[]{:S(2)}) async-start(), calls=%async_computation | async-start | bytes 3244032 | tf_op jit(solution)/shard_map/all_gather | solution.py:87
  11.5 243.9 %all-reduce.2.cloned.1.call-start = ((), (), s32[]{:S(2)}) async-start(), calls=%async_computation.1 | async-start | bytes 393216 | tf_op jit(solution)/shard_map/psum | solution.py:112
  157.1 2.6 copy-start.6
  159.7 16.1 %copy-start.1 = (bf16[16,24,256]{2,1,0:T(8,128)(2,1)S(1)}, bf16[16,24,256]{2,1,0:T(8,128)(2,1)}, u32[]{:S(2)}) copy-start(bf16[16,24,256]{2,1,0:T(8,128)(2,1)} %param.11) | copy-start | bytes 589828
  175.8 2.6 collective-permute-start
  177.1 5.7 %collective-permute-start.1 = (bf16[3,24,256]{2,1,0:T(8,128)(2,1)S(1)}, bf16[3,24,256]{2,1,0:T(8,128)(2,1)S(1)}, u32[]{:S(2)}, u32[]{:S(2)}) collective-permute-start(bf16[3,24,256]{2,1,0:T(8,128)(2,1)S(1)} %get-tuple-element.12), channel_id=1, source_target_pairs={{128,0},{256,128},{384,256},{129,1},{257,129},{385,257},{130,2},{2... | collective-permute-start | bytes 110600 | tf_op jit(solution)/shard_map/ppermute | solution.py:23
  182.9 6.4 %collective-permute-start.2 = (bf16[22,3,256]{2,1,0:T(4,128)(2,1)S(1)}, bf16[22,3,256]{2,1,0:T(4,128)(2,1)S(1)}, u32[]{:S(2)}, u32[]{:S(2)}) collective-permute-start(bf16[22,3,256]{2,1,0:T(4,128)(2,1)S(1)} %get-tuple-element.9), channel_id=1, source_target_pairs={{0,4},{4,8},{8,12},{12,16},{16,20},{20,24},{24,28},{28,32},{32,36}... | collective-permute-start | bytes 101384 | tf_op jit(solution)/shard_map/ppermute | solution.py:22
  187.3 6.8 %collective-permute-start.3 = (bf16[22,3,256]{2,1,0:T(4,128)(2,1)S(1)}, bf16[22,3,256]{2,1,0:T(4,128)(2,1)S(1)}, u32[]{:S(2)}, u32[]{:S(2)}) collective-permute-start(bf16[22,3,256]{2,1,0:T(4,128)(2,1)S(1)} %get-tuple-element.10), channel_id=1, source_target_pairs={{4,0},{8,4},{12,8},{16,12},{20,16},{24,20},{28,24},{32,28},{36,32}... | collective-permute-start | bytes 101384 | tf_op jit(solution)/shard_map/ppermute | solution.py:23
  194.3 3.2 %copy-start.7 = (f32[256]{0:T(256)S(1)}, f32[256]{0:T(256)}, u32[]{:S(2)}) copy-start(f32[256]{0:T(256)} %param.18) | copy-start | bytes 3076
  194.3 3.6 %copy-start.5 = (bf16[256,256]{1,0:T(8,128)(2,1)S(1)}, bf16[256,256]{1,0:T(8,128)(2,1)}, u32[]{:S(2)}) copy-start(bf16[256,256]{1,0:T(8,128)(2,1)} %param.20) | copy-start | bytes 393220
  197.9 1.8 copy-start.4
Sparse Core Ops, SparseCore 0:
  11.7 140.6 all-gather.2
  199.8 55.6 all-reduce.1
